TPU v7x, 32 devices: a whole 2x2x4 slice. The times are simulated.
32 devices in a mesh: tgt: 8 (over z, y), src: 4 (over x, core).
Axes of the slice: x: 2, y: 2, z: 4, core: 2. Of those that a mesh axis runs over, the one named last changes fastest.
Arguments:
- coefficients: bfloat16 [32, 4, 512, 512], P('tgt', 'src'), may hold values from -1.5 to 1.5
- factors: bfloat16 [3, 32, 4, 512, 512], P(None, 'tgt', 'src'), may hold values from -0.25 to 0.25
Outputs:
- potentials: float32 [32, 2, 256, 512], P('tgt', None, 'src')
All inputs are finite; a program needn't handle non-finite values.
Results may differ from a plain program's by a relative error of at most 0.013.
Values may be sent and summed in bfloat16 or wider, within the bound.
A program may use at most 64 MiB of HBM per device.

v0:
```python
import functools

import jax
import jax.numpy as jnp
from jax import lax
from jax.experimental import pallas as pl
from jax.experimental.pallas import tpu as pltpu
from jax.sharding import PartitionSpec as P

PARTS = 4
LAGS = (3, 7, 10)
AHEAD = 6


def kernel(sizes, coef_ref, fact_ref, out_ref, *scratch):
    n_tgt, n_src, levels, blocks, half, width, parts, lags, ahead = sizes
    chunks, rows = blocks * parts, half // n_src
    fact, current, sends, part, inbox, low_send, low_recv = scratch[:7]
    load_sem, coef_sem, lev_send, lev_recv, src_send, src_recv, low_sems = scratch[7:]
    me = lax.axis_index("tgt")
    src = lax.axis_index("src")
    bits = n_tgt.bit_length() - 1

    def partner(level):
        step = 1 << level % bits
        return me + step * (1 - 2 * ((me // step) % 2))

    def peer(k):
        return (src + k) % n_src

    def load(level, block):
        return pltpu.make_async_copy(
            fact_ref.at[level, block], fact.at[level, block], load_sem.at[level, block]
        )

    def load_coef(c):
        return pltpu.make_async_copy(
            coef_ref.at[c // parts, :, pl.ds(pl.multiple_of((c % parts) * width, width), width)],
            current.at[0, c],
            coef_sem.at[c],
        )

    for b in range(blocks):
        load(0, b).start()
        for h in range(parts):
            load_coef(b * parts + h).start()
    for level in range(1, levels):
        for b in range(blocks):
            load(level, b).start()

    barrier = pltpu.get_barrier_semaphore()
    shifts = sorted({level % bits for level in range(levels)})
    for shift in shifts:
        pl.semaphore_signal(
            barrier, inc=1, device_id={"tgt": partner(shift)}, device_id_type=pl.DeviceIdType.MESH
        )
    for k in range(1, n_src):
        pl.semaphore_signal(
            barrier, inc=1, device_id={"src": peer(k)}, device_id_type=pl.DeviceIdType.MESH
        )

    def exchange(level, c):
        return pltpu.make_async_remote_copy(
            src_ref=sends.at[level, c],
            dst_ref=current.at[level + 1, c, pl.ds(half, half)],
            send_sem=lev_send.at[level, c],
            recv_sem=lev_recv.at[level, c],
            device_id={"tgt": partner(level)},
            device_id_type=pl.DeviceIdType.MESH,
        )

    def scatter(k, c):
        return pltpu.make_async_remote_copy(
            src_ref=part.at[c, peer(k)],
            dst_ref=inbox.at[c, k],
            send_sem=src_send.at[c, k],
            recv_sem=src_recv.at[c, k],
            device_id={"src": peer(k)},
            device_id_type=pl.DeviceIdType.MESH,
        )

    def lower(c):
        return pltpu.make_async_remote_copy(
            src_ref=low_send.at[c],
            dst_ref=low_recv.at[c],
            send_sem=low_sems.at[0, c],
            recv_sem=low_sems.at[1, c],
            device_id={"tgt": partner(levels - 1)},
            device_id_type=pl.DeviceIdType.MESH,
        )

    def write(side, c, value):
        columns = pl.ds(pl.multiple_of((c % parts) * width, width), width)
        out_ref[c // parts, side, :, columns] = value

    def level_stage(level, c, before_send=None):
        if level:
            exchange(level - 1, c).wait_recv()

        def blend(rows):
            return jnp.dot(
                fact[level, c // parts, rows], current[level, c], preferred_element_type=jnp.float32
            ).astype(jnp.bfloat16)

        if level < levels - 1:
            sends[level, c] = blend(pl.ds(half, half))
            if before_send is not None:
                before_send()
            exchange(level, c).start()
            current[level + 1, c, :half] = blend(pl.ds(0, half))
        else:
            blended = blend(pl.ds(0, 2 * half))
            for j in range(n_src):
                part[c, j, 0] = blended[j * rows : (j + 1) * rows]
                part[c, j, 1] = blended[half + j * rows : half + (j + 1) * rows]
            for k in range(1, n_src):
                scatter(k, c).start()

    def sum_stage(c):
        total = part[c, src].astype(jnp.float32)
        for k in range(1, n_src):
            scatter(k, c).wait_recv()
            total += inbox[c, k].astype(jnp.float32)
        low_send[c] = total[1].astype(jnp.bfloat16)
        lower(c).start()
        write(0, c, total[0])

    def last_stage(c):
        lower(c).wait_recv()
        write(1, c, low_recv[c].astype(jnp.float32))

    def first(c, before_send=None):
        load_coef(c).wait()

        @pl.when(c % parts == 0)
        def _():
            load(0, c // parts).wait()

        level_stage(0, c, before_send)

    def later(level, c):
        @pl.when(c % parts == 0)
        def _():
            load(level, c // parts).wait()

        level_stage(level, c)

    def looped(c, carry):
        first(c)
        return carry

    first(jnp.int32(0), lambda: pl.semaphore_wait(barrier, len(shifts) + n_src - 1))
    lax.fori_loop(1, ahead, looped, 0)

    stages = [functools.partial(later, level) for level in range(1, levels)]
    stages += [sum_stage, last_stage]
    if ahead < chunks:
        stages.append(first)

    def step(i, carry):
        for stage, lag in zip(stages, (0,) + lags + (-ahead,)):
            c = i - lag

            @pl.when(jnp.logical_and(c >= 0, c < chunks))
            def _():
                stage(c)

        return carry

    lax.fori_loop(0, chunks + lags[-1], step, 0)

    def finish(c, carry):
        for level in range(levels - 1):
            exchange(level, c).wait_send()
        for k in range(1, n_src):
            scatter(k, c).wait_send()
        lower(c).wait_send()
        return carry

    lax.fori_loop(0, chunks, finish, 0)


def local(n_tgt, n_src, coefficients, factors):
    levels, blocks = factors.shape[0], factors.shape[1]
    size, columns = coefficients.shape[2], coefficients.shape[3]
    half, width = size // 2, columns // PARTS
    chunks, rows = blocks * PARTS, half // n_src
    dma = pltpu.SemaphoreType.DMA
    bf16 = jnp.bfloat16
    return pl.pallas_call(
        functools.partial(
            kernel, (n_tgt, n_src, levels, blocks, half, width, PARTS, LAGS, min(AHEAD, chunks))
        ),
        out_shape=pltpu.VMEM((blocks, 2, rows, columns), jnp.float32),
        in_specs=[pl.BlockSpec(memory_space=pl.ANY)] * 2,
        out_specs=pl.BlockSpec(memory_space=pltpu.VMEM),
        scratch_shapes=[
            pltpu.VMEM((levels, blocks, size, size), bf16),
            pltpu.VMEM((levels, chunks, size, width), bf16),
            pltpu.VMEM((levels - 1, chunks, half, width), bf16),
            pltpu.VMEM((chunks, n_src, 2, rows, width), bf16),
            pltpu.VMEM((chunks, n_src, 2, rows, width), bf16),
            pltpu.VMEM((chunks, rows, width), bf16),
            pltpu.VMEM((chunks, rows, width), bf16),
            dma((levels, blocks)),
            dma((chunks,)),
            dma((levels - 1, chunks)),
            dma((levels - 1, chunks)),
            dma((chunks, n_src)),
            dma((chunks, n_src)),
            dma((2, chunks)),
        ],
        compiler_params=pltpu.CompilerParams(collective_id=0, has_side_effects=True),
    )(coefficients[:, 0], factors[:, :, 0])


def solution(mesh):
    placed = (P("tgt", "src", None, None), P(None, "tgt", "src", None, None))
    return jax.shard_map(
        functools.partial(local, mesh.shape["tgt"], mesh.shape["src"]),
        mesh=mesh,
        in_specs=placed,
        out_specs=P("tgt", None, "src", None),
        check_vma=False,
    )
```

profile of v0, /device:TPU:0, one launch (start us, length us, event | category | flops | bytes accessed | tf_op | source)
XLA Modules:
  0.0 46.6 jit_solution(5144252803197296064)
XLA Ops:
  0.0 45.6 %shard_map.28 = f32[4,2,64,512]{3,2,1,0:T(8,128)S(1)} custom-call(bf16[4,512,512]{2,1,0:T(8,128)(2,1)} %bitcast.3, bf16[3,4,512,512]{3,2,1,0:T(8,128)(2,1)} %bitcast.2), custom_call_target="tpu_custom_call" | custom-call | tf_op jit(solution)/shard_map/pallas_call | solution.py:190
  45.6 1.0 %copy.4 = f32[4,2,64,512]{3,2,1,0:T(8,128)} copy(f32[4,2,64,512]{3,2,1,0:T(8,128)S(1)} %shard_map.28) | data formatting | bytes 2097152
where the time goes:
time: 46.8 us; the launch traced here: 46.6 us
  Pallas kernels  45.6 us (97%)
  local copies, waits for them, and re-layouts  0.97 us (2%)
    pallas_call x1, Pallas kernels, local(): pl.pallas_call(functools.partial(kernel, (n_tgt, n_src, levels, blocks, h...  45.6 us
    unnamed x1, local copies, waits for them, and re-layouts  0.97 us

commit v1 on v0

v1 whole, which is shorter than its diff:
```python
import functools

import jax
import jax.numpy as jnp
from jax import lax
from jax.experimental import pallas as pl
from jax.experimental.pallas import tpu as pltpu
from jax.sharding import PartitionSpec as P

PARTS = 4
READY = 1
LAGS = (3, 7)
HOLD = 6


def kernel(sizes, coef_ref, fact_ref, out_ref, *scratch):
    n_tgt, n_src, levels, blocks, half, width, parts, lags, ready, hold = sizes
    chunks, rows = blocks * parts, half // n_src
    coef, fact, current, sends, part, inbox, low_send, low_recv = scratch[:8]
    first_sem, load_sem, lev_send, lev_recv, src_send, src_recv, low_sent, low_got = scratch[8:]
    me = lax.axis_index("tgt")
    src = lax.axis_index("src")
    bits = n_tgt.bit_length() - 1

    def partner(level):
        step = 1 << level % bits
        return me + step * (1 - 2 * ((me // step) % 2))

    def peer(k):
        return (src + k) % n_src

    def load_first(b):
        return (
            pltpu.make_async_copy(coef_ref.at[b], coef.at[b], first_sem.at[0, b]),
            pltpu.make_async_copy(fact_ref.at[0, b], fact.at[0, b], first_sem.at[1, b]),
        )

    def load(level):
        return pltpu.make_async_copy(fact_ref.at[level], fact.at[level], load_sem.at[level - 1])

    barrier = pltpu.get_barrier_semaphore()
    shifts = sorted({level % bits for level in range(levels)})
    for shift in shifts:
        pl.semaphore_signal(
            barrier, inc=1, device_id={"tgt": partner(shift)}, device_id_type=pl.DeviceIdType.MESH
        )
    for k in range(1, n_src):
        pl.semaphore_signal(
            barrier, inc=1, device_id={"src": peer(k)}, device_id_type=pl.DeviceIdType.MESH
        )

    for b in range(blocks):
        for copy in load_first(b):
            copy.start()
    for level in range(1, levels):
        load(level).start()

    def exchange(level, c):
        return pltpu.make_async_remote_copy(
            src_ref=sends.at[level, c],
            dst_ref=current.at[level, c, pl.ds(half, half)],
            send_sem=lev_send.at[0],
            recv_sem=lev_recv.at[level, c],
            device_id={"tgt": partner(level)},
            device_id_type=pl.DeviceIdType.MESH,
        )

    def scatter(k, c):
        return pltpu.make_async_remote_copy(
            src_ref=part.at[c, peer(k)],
            dst_ref=inbox.at[c, k - 1],
            send_sem=src_send.at[0],
            recv_sem=src_recv.at[c],
            device_id={"src": peer(k)},
            device_id_type=pl.DeviceIdType.MESH,
        )

    def lower(c):
        return pltpu.make_async_remote_copy(
            src_ref=low_send.at[c],
            dst_ref=low_recv.at[c],
            send_sem=low_sent.at[0],
            recv_sem=low_got.at[c // parts],
            device_id={"tgt": partner(levels - 1)},
            device_id_type=pl.DeviceIdType.MESH,
        )

    def whole(ref, sem):
        return pltpu.make_async_copy(ref, ref, sem)

    def columns(c):
        return pl.ds(pl.multiple_of((c % parts) * width, width), width)

    def write(side, c, value):
        out_ref[c // parts, side, :, columns(c)] = value

    def blend(level, c, rows):
        value = current[level - 1, c] if level else coef[c // parts, :, columns(c)]
        return jnp.dot(
            fact[level, c // parts, rows], value, preferred_element_type=jnp.float32
        ).astype(jnp.bfloat16)

    upper_rows, lower_rows = pl.ds(0, half), pl.ds(half, half)

    def wait_factor(level, c):
        @pl.when(c == 0)
        def _():
            load(level).wait()

    def prepare(c, carry):
        @pl.when(c % parts == 0)
        def _():
            for copy in load_first(c // parts):
                copy.wait()

        sends[0, c] = blend(0, c, lower_rows)
        return carry

    def send_first(c, carry):
        exchange(0, c).start()
        return carry

    def prepare_send(c, carry):
        prepare(c, carry)
        return send_first(c, carry)

    def middle(level, c):
        current[level - 1, c, :half] = blend(level - 1, c, upper_rows)
        wait_factor(level, c)
        exchange(level - 1, c).wait_recv()
        sends[level, c] = blend(level, c, lower_rows)
        exchange(level, c).start()

    def final(c):
        level = levels - 1
        current[level - 1, c, :half] = blend(level - 1, c, upper_rows)
        wait_factor(level, c)
        exchange(level - 1, c).wait_recv()
        blended = blend(level, c, pl.ds(0, 2 * half))
        for j in range(n_src):
            part[c, j, 0] = blended[j * rows : (j + 1) * rows]
            part[c, j, 1] = blended[half + j * rows : half + (j + 1) * rows]
        for k in range(1, n_src):
            scatter(k, c).start()

    def sum_stage(c):
        total = part[c, src].astype(jnp.float32)
        whole(inbox.at[c], src_recv.at[c]).wait()
        for k in range(1, n_src):
            total += inbox[c, k - 1].astype(jnp.float32)
        low_send[c] = total[1].astype(jnp.bfloat16)
        write(0, c, total[0])

    lax.fori_loop(0, ready, prepare, 0)
    pl.semaphore_wait(barrier, len(shifts) + n_src - 1)
    lax.fori_loop(0, ready, send_first, 0)
    lax.fori_loop(ready, chunks, prepare_send, 0)

    def sum_and_send(i, c):
        sum_stage(c)

        @pl.when(jnp.logical_or(c < hold, i >= chunks - 1))
        def _():
            lower(c).start()

    def release(c, carry):
        lower(c).start()
        return carry

    stages = [functools.partial(middle, level) for level in range(1, levels - 1)] + [final]
    lag_sum = lags[-1]

    def step(i, carry):
        for stage, lag in zip(stages, (0,) + lags):
            c = i - lag

            @pl.when(jnp.logical_and(c >= 0, c < chunks))
            def _():
                stage(c)

        @pl.when(i == chunks - 1)
        def _():
            lax.fori_loop(hold, max(hold, chunks - 1 - lag_sum), release, 0)

        c = i - lag_sum

        @pl.when(jnp.logical_and(c >= 0, c < chunks))
        def _():
            sum_and_send(i, c)

        return carry

    lax.fori_loop(0, chunks + lag_sum, step, 0)

    whole(sends, lev_send.at[0]).wait()
    whole(inbox, src_send.at[0]).wait()
    whole(low_send, low_sent.at[0]).wait()

    def last_stage(b, carry):
        group = pl.ds(b * parts, parts)
        whole(low_recv.at[group], low_got.at[b]).wait()
        for h in range(parts):
            out_ref[b, 1, :, h * width : (h + 1) * width] = low_recv[b * parts + h].astype(jnp.float32)
        return carry

    lax.fori_loop(0, blocks, last_stage, 0)


def local(n_tgt, n_src, coefficients, factors):
    levels, blocks = factors.shape[0], factors.shape[1]
    size, columns = coefficients.shape[2], coefficients.shape[3]
    half, width = size // 2, columns // PARTS
    chunks, rows = blocks * PARTS, half // n_src
    dma = pltpu.SemaphoreType.DMA
    bf16 = jnp.bfloat16
    return pl.pallas_call(
        functools.partial(
            kernel,
            (n_tgt, n_src, levels, blocks, half, width, PARTS, LAGS, min(READY, chunks), min(HOLD, chunks)),
        ),
        out_shape=pltpu.VMEM((blocks, 2, rows, columns), jnp.float32),
        in_specs=[pl.BlockSpec(memory_space=pl.ANY)] * 2,
        out_specs=pl.BlockSpec(memory_space=pltpu.VMEM),
        scratch_shapes=[
            pltpu.VMEM((blocks, size, columns), bf16),
            pltpu.VMEM((levels, blocks, size, size), bf16),
            pltpu.VMEM((levels - 1, chunks, size, width), bf16),
            pltpu.VMEM((levels - 1, chunks, half, width), bf16),
            pltpu.VMEM((chunks, n_src, 2, rows, width), bf16),
            pltpu.VMEM((chunks, n_src - 1, 2, rows, width), bf16),
            pltpu.VMEM((chunks, rows, width), bf16),
            pltpu.VMEM((chunks, rows, width), bf16),
            dma((2, blocks)),
            dma((levels - 1,)),
            dma((1,)),
            dma((levels - 1, chunks)),
            dma((1,)),
            dma((chunks,)),
            dma((1,)),
            dma((blocks,)),
        ],
        compiler_params=pltpu.CompilerParams(collective_id=0, has_side_effects=True),
    )(coefficients[:, 0], factors[:, :, 0])


def solution(mesh):
    placed = (P("tgt", "src", None, None), P(None, "tgt", "src", None, None))
    return jax.shard_map(
        functools.partial(local, mesh.shape["tgt"], mesh.shape["src"]),
        mesh=mesh,
        in_specs=placed,
        out_specs=P("tgt", None, "src", None),
        check_vma=False,
    )
```

time: 46.8 us -> 44.4 us (0.949)
  Pallas kernels: 45.6 us -> 43.3 us
    pallas_call x1, Pallas kernels: 45.6 us -> 43.3 us  [local(): pl.pallas_call(functools.partial(kernel, (n_tgt, n_src, levels, blocks, h...]
where the time goes in v1:
time: 44.4 us; the launch traced here: 44.3 us
  Pallas kernels  43.3 us (98%)
  local copies, waits for them, and re-layouts  0.97 us (2%)
    pallas_call x1, Pallas kernels, local(): pl.pallas_call(functools.partial(kernel, (n_tgt, n_src, levels, blocks, h...  43.3 us
    unnamed x1, local copies, waits for them, and re-layouts  0.97 us

profile of v1, /device:TPU:0, one launch (start us, length us, event | category | flops | bytes accessed | tf_op | source)
XLA Modules:
  0.0 44.3 jit_solution(15130909730309177168)
XLA Ops:
  0.0 43.3 %shard_map.28 = f32[4,2,64,512]{3,2,1,0:T(8,128)S(1)} custom-call(bf16[4,512,512]{2,1,0:T(8,128)(2,1)} %bitcast.3, bf16[3,4,512,512]{3,2,1,0:T(8,128)(2,1)} %bitcast.2), custom_call_target="tpu_custom_call" | custom-call | tf_op jit(solution)/shard_map/pallas_call | solution.py:216
  43.3 1.0 %copy.4 = f32[4,2,64,512]{3,2,1,0:T(8,128)} copy(f32[4,2,64,512]{3,2,1,0:T(8,128)S(1)} %shard_map.28) | data formatting | bytes 2097152

commit v2 on v1

--- a/solution.py
+++ b/solution.py
@@ -9,7 +9,7 @@
 
 PARTS = 4
 READY = 1
-LAGS = (3, 7)
+LAGS = (3, 8)
 HOLD = 6
 
 
@@ -156,10 +156,14 @@
     lax.fori_loop(0, ready, send_first, 0)
     lax.fori_loop(ready, chunks, prepare_send, 0)
 
+    near, far = 1 << (levels - 2) % bits, 1 << (levels - 1) % bits
+    inner = (me // near) % 2 != (me // far) % 2
+    held = jnp.where(inner, 16, 0)
+
     def sum_and_send(i, c):
         sum_stage(c)
 
-        @pl.when(jnp.logical_or(c < hold, i >= chunks - 1))
+        @pl.when(jnp.logical_or(c < held, i >= chunks - 1))
         def _():
             lower(c).start()
 
@@ -180,7 +184,7 @@
 
         @pl.when(i == chunks - 1)
         def _():
-            lax.fori_loop(hold, max(hold, chunks - 1 - lag_sum), release, 0)
+            lax.fori_loop(held, jnp.maximum(held, chunks - 1 - lag_sum), release, 0)
 
         c = i - lag_sum
 

time: 44.4 us -> 43.5 us (0.980)
  Pallas kernels: 43.3 us -> 42.4 us
    pallas_call x1, Pallas kernels: 43.3 us -> 42.4 us  [local(): pl.pallas_call(functools.partial(kernel, (n_tgt, n_src, levels, blocks, h...]
where the time goes in v2:
time: 43.5 us; the launch traced here: 43.4 us
  Pallas kernels  42.4 us (97%)
  local copies, waits for them, and re-layouts  0.97 us (2%)
    pallas_call x1, Pallas kernels, local(): pl.pallas_call(functools.partial(kernel, (n_tgt, n_src, levels, blocks, h...  42.4 us
    unnamed x1, local copies, waits for them, and re-layouts  0.97 us

profile of v2, /device:TPU:0, one launch (start us, length us, event | category | flops | bytes accessed | tf_op | source)
XLA Modules:
  0.0 43.4 jit_solution(9913663024375028763)
XLA Ops:
  0.0 42.4 %shard_map.28 = f32[4,2,64,512]{3,2,1,0:T(8,128)S(1)} custom-call(bf16[4,512,512]{2,1,0:T(8,128)(2,1)} %bitcast.3, bf16[3,4,512,512]{3,2,1,0:T(8,128)(2,1)} %bitcast.2), custom_call_target="tpu_custom_call" | custom-call | tf_op jit(solution)/shard_map/pallas_call | solution.py:220
  42.4 1.0 %copy.4 = f32[4,2,64,512]{3,2,1,0:T(8,128)} copy(f32[4,2,64,512]{3,2,1,0:T(8,128)S(1)} %shard_map.28) | data formatting | bytes 2097152

commit v3 on v2

--- a/solution.py
+++ b/solution.py
@@ -10,11 +10,10 @@
 PARTS = 4
 READY = 1
 LAGS = (3, 8)
-HOLD = 6
 
 
 def kernel(sizes, coef_ref, fact_ref, out_ref, *scratch):
-    n_tgt, n_src, levels, blocks, half, width, parts, lags, ready, hold = sizes
+    n_tgt, n_src, levels, blocks, half, width, parts, lags, ready = sizes
     chunks, rows = blocks * parts, half // n_src
     coef, fact, current, sends, part, inbox, low_send, low_recv = scratch[:8]
     first_sem, load_sem, lev_send, lev_recv, src_send, src_recv, low_sent, low_got = scratch[8:]
@@ -143,12 +142,13 @@
         for k in range(1, n_src):
             scatter(k, c).start()
 
-    def sum_stage(c):
+    def sum_stage(c, send):
         total = part[c, src].astype(jnp.float32)
         whole(inbox.at[c], src_recv.at[c]).wait()
         for k in range(1, n_src):
             total += inbox[c, k - 1].astype(jnp.float32)
         low_send[c] = total[1].astype(jnp.bfloat16)
+        send()
         write(0, c, total[0])
 
     lax.fori_loop(0, ready, prepare, 0)
@@ -158,14 +158,15 @@
 
     near, far = 1 << (levels - 2) % bits, 1 << (levels - 1) % bits
     inner = (me // near) % 2 != (me // far) % 2
-    held = jnp.where(inner, 16, 0)
+    held = jnp.where(inner, chunks, 0)
 
     def sum_and_send(i, c):
-        sum_stage(c)
-
-        @pl.when(jnp.logical_or(c < held, i >= chunks - 1))
-        def _():
-            lower(c).start()
+        def send():
+            @pl.when(jnp.logical_or(c < held, i >= chunks - 1))
+            def _():
+                lower(c).start()
+
+        sum_stage(c, send)
 
     def release(c, carry):
         lower(c).start()
@@ -195,10 +196,6 @@
         return carry
 
     lax.fori_loop(0, chunks + lag_sum, step, 0)
-
-    whole(sends, lev_send.at[0]).wait()
-    whole(inbox, src_send.at[0]).wait()
-    whole(low_send, low_sent.at[0]).wait()
 
     def last_stage(b, carry):
         group = pl.ds(b * parts, parts)
@@ -208,6 +205,9 @@
         return carry
 
     lax.fori_loop(0, blocks, last_stage, 0)
+    whole(sends, lev_send.at[0]).wait()
+    whole(inbox, src_send.at[0]).wait()
+    whole(low_send, low_sent.at[0]).wait()
 
 
 def local(n_tgt, n_src, coefficients, factors):
@@ -220,7 +220,7 @@
     return pl.pallas_call(
         functools.partial(
             kernel,
-            (n_tgt, n_src, levels, blocks, half, width, PARTS, LAGS, min(READY, chunks), min(HOLD, chunks)),
+            (n_tgt, n_src, levels, blocks, half, width, PARTS, LAGS, min(READY, chunks)),
         ),
         out_shape=pltpu.VMEM((blocks, 2, rows, columns), jnp.float32),
         in_specs=[pl.BlockSpec(memory_space=pl.ANY)] * 2,

time: 43.5 us -> 43.4 us (level)
  no operation moved by 1% of the time
where the time goes in v3:
time: 43.4 us; the launch traced here: 43.3 us
  Pallas kernels  42.3 us (97%)
  local copies, waits for them, and re-layouts  0.97 us (2%)
    pallas_call x1, Pallas kernels, local(): pl.pallas_call(functools.partial(kernel, (n_tgt, n_src, levels, blocks, h...  42.3 us
    unnamed x1, local copies, waits for them, and re-layouts  0.97 us

profile of v3, /device:TPU:0, one launch (start us, length us, event | category | flops | bytes accessed | tf_op | source)
XLA Modules:
  0.0 43.3 jit_solution(6382744582111667692)
XLA Ops:
  0.0 42.3 %shard_map.28 = f32[4,2,64,512]{3,2,1,0:T(8,128)S(1)} custom-call(bf16[4,512,512]{2,1,0:T(8,128)(2,1)} %bitcast.3, bf16[3,4,512,512]{3,2,1,0:T(8,128)(2,1)} %bitcast.2), custom_call_target="tpu_custom_call" | custom-call | tf_op jit(solution)/shard_map/pallas_call | solution.py:220
  42.3 1.0 %copy.4 = f32[4,2,64,512]{3,2,1,0:T(8,128)} copy(f32[4,2,64,512]{3,2,1,0:T(8,128)S(1)} %shard_map.28) | data formatting | bytes 2097152
